TPU v7x, 32 devices: a whole 2x2x4 slice. The times are simulated.
32 devices in a mesh: lat: 4 (over y, x), lon: 8 (over z, core).
Axes of the slice: x: 2, y: 2, z: 4, core: 2. Of those that a mesh axis runs over, the one named last changes fastest.
Arguments:
- fields: bfloat16 [1, 64, 64, 768], P(None, 'lat', 'lon'), may hold values from -6 to 6
- spec_cotangent: bfloat16 [2, 1, 64, 32, 768], P(None, None, 'lon', 'lat'), may hold values from -6 to 6
- inner_kernel: bfloat16 [2, 8, 96, 96], replicated, may hold values from -0.4375 to 0.4375
- inner_offset: float32 [2, 8, 96], replicated, may hold values from -3 to 3
- outer_kernel: bfloat16 [2, 8, 96, 96], replicated, may hold values from -0.4375 to 0.4375
- outer_offset: float32 [2, 8, 96], replicated, may hold values from -3 to 3
Outputs:
- filtered: float32 [2, 1, 64, 32, 768], P(None, None, 'lon', 'lat')
- inner_kernel_grad: float32 [2, 8, 96, 96], replicated
- inner_offset_grad: float32 [2, 8, 96], replicated
- outer_kernel_grad: float32 [2, 8, 96, 96], replicated
- outer_offset_grad: float32 [2, 8, 96], replicated
All inputs are finite; a program needn't handle non-finite values.
Results may differ from a plain program's by a relative error of at most 0.0072.
Values may be sent and summed in bfloat16 or wider, within the bound.
A program may use at most 64 MiB of HBM per device.

v0:
```python
import math
import jax
import jax.numpy as jnp
from jax import lax
from jax.sharding import PartitionSpec as P

shrink_level = 0.1
gelu_coeff = 0.7978845608028654
precise = lax.Precision.HIGHEST


def dft_tables(length, columns):
    points = jnp.arange(length, dtype=jnp.int32)
    orders = jnp.arange(columns, dtype=jnp.int32)
    product = points[:, None] * orders[None, :] % length
    angles = product.astype(jnp.float32) * (2.0 * math.pi / length)
    factor = 1.0 / math.sqrt(length)
    return (jnp.cos(angles) * factor, jnp.sin(angles) * factor)


def shrink(values):
    return values - shrink_level * jnp.tanh(values / shrink_level)


def shrink_slope(values):
    level = jnp.tanh(values / shrink_level)
    return level * level


def gelu_value(values):
    inner = gelu_coeff * (values + 0.044715 * values * values * values)
    return 0.5 * values * (1.0 + jnp.tanh(inner))


def gelu_slope(values):
    inner = gelu_coeff * (values + 0.044715 * values * values * values)
    level = jnp.tanh(inner)
    return 0.5 * (1.0 + level) + 0.5 * values * (1.0 - level * level) * gelu_coeff * (
        1.0 + 3.0 * 0.044715 * values * values
    )


def mixing(operand, kernel):
    return jnp.einsum("rnb,nbc->rnc", operand, kernel, preferred_element_type=jnp.float32)


def backmix(operand, kernel):
    return jnp.einsum("rnc,nbc->rnb", operand, kernel, preferred_element_type=jnp.float32)


def crossed(operand, second):
    return jnp.einsum("rnb,rnc->nbc", operand, second, preferred_element_type=jnp.float32)


def block_filter(spectrum, cotangent, inner_kernel, inner_offset, outer_kernel, outer_offset):
    spec_real, spec_imag = (spectrum[0], spectrum[1])
    pre_real = (
        mixing(spec_real, inner_kernel[0]) - mixing(spec_imag, inner_kernel[1]) + inner_offset[0]
    )
    pre_imag = (
        mixing(spec_imag, inner_kernel[0]) + mixing(spec_real, inner_kernel[1]) + inner_offset[1]
    )
    hid_real = gelu_value(pre_real).astype(jnp.bfloat16)
    hid_imag = gelu_value(pre_imag).astype(jnp.bfloat16)
    out_real = (
        mixing(hid_real, outer_kernel[0]) - mixing(hid_imag, outer_kernel[1]) + outer_offset[0]
    )
    out_imag = (
        mixing(hid_imag, outer_kernel[0]) + mixing(hid_real, outer_kernel[1]) + outer_offset[1]
    )
    filtered = jnp.stack([shrink(out_real), shrink(out_imag)])
    back_real = (cotangent[0].astype(jnp.float32) * shrink_slope(out_real)).astype(jnp.bfloat16)
    back_imag = (cotangent[1].astype(jnp.float32) * shrink_slope(out_imag)).astype(jnp.bfloat16)
    outer_grad = jnp.stack(
        [
            crossed(hid_real, back_real) + crossed(hid_imag, back_imag),
            crossed(hid_real, back_imag) - crossed(hid_imag, back_real),
        ]
    )
    outer_bias = jnp.stack(
        [
            jnp.sum(back_real, axis=0, dtype=jnp.float32),
            jnp.sum(back_imag, axis=0, dtype=jnp.float32),
        ]
    )
    grad_real = (
        (backmix(back_real, outer_kernel[0]) + backmix(back_imag, outer_kernel[1]))
        * gelu_slope(pre_real)
    ).astype(jnp.bfloat16)
    grad_imag = (
        (backmix(back_imag, outer_kernel[0]) - backmix(back_real, outer_kernel[1]))
        * gelu_slope(pre_imag)
    ).astype(jnp.bfloat16)
    inner_grad = jnp.stack(
        [
            crossed(spec_real, grad_real) + crossed(spec_imag, grad_imag),
            crossed(spec_real, grad_imag) - crossed(spec_imag, grad_real),
        ]
    )
    inner_bias = jnp.stack(
        [
            jnp.sum(grad_real, axis=0, dtype=jnp.float32),
            jnp.sum(grad_imag, axis=0, dtype=jnp.float32),
        ]
    )
    return (filtered, (inner_grad, inner_bias, outer_grad, outer_bias))


def per_device(fields, spec_cotangent, inner_kernel, inner_offset, outer_kernel, outer_offset):
    lat_devices = lax.axis_size("lat")
    lon_devices = lax.axis_size("lon")
    conditions = fields.shape[0]
    height = fields.shape[1] * lat_devices
    width = fields.shape[2] * lon_devices
    wavenumbers = width // 2
    cosine_rows, sine_rows = dft_tables(height, height)
    cosine_cols, sine_cols = dft_tables(width, wavenumbers)
    arriving = lax.all_to_all(fields, "lat", split_axis=3, concat_axis=1, tiled=True)
    shape_in = arriving.shape
    floats = arriving.astype(jnp.float32).reshape(
        shape_in[0], shape_in[1], shape_in[2] * shape_in[3]
    )
    real_part = jnp.einsum("bhx,hm->bmx", floats, cosine_rows, precision=precise)
    imag_part = -jnp.einsum("bhx,hm->bmx", floats, sine_rows, precision=precise)
    spec_rows = jnp.stack([real_part, imag_part]).reshape((2,) + shape_in)
    arriving = lax.all_to_all(spec_rows, "lon", split_axis=2, concat_axis=3, tiled=True)
    real_part = jnp.einsum(
        "bhwd,wk->bhkd", arriving[0], cosine_cols, precision=precise
    ) + jnp.einsum("bhwd,wk->bhkd", arriving[1], sine_cols, precision=precise)
    imag_part = jnp.einsum(
        "bhwd,wk->bhkd", arriving[1], cosine_cols, precision=precise
    ) - jnp.einsum("bhwd,wk->bhkd", arriving[0], sine_cols, precision=precise)
    spec_half = jnp.stack([real_part, imag_part]).astype(jnp.bfloat16)
    spectrum = lax.all_to_all(spec_half, "lat", split_axis=3, concat_axis=4, tiled=True)
    blocks = inner_kernel.shape[1]
    block_width = inner_kernel.shape[2]
    local_shape = spectrum.shape
    flat_spec = spectrum.reshape(2, -1, blocks, block_width)
    flat_cot = spec_cotangent.reshape(2, -1, blocks, block_width)
    filtered, gradients = block_filter(
        flat_spec, flat_cot, inner_kernel, inner_offset, outer_kernel, outer_offset
    )
    totals = lax.psum((gradients[0], gradients[1], gradients[2], gradients[3]), ("lat", "lon"))
    normalizer = 1.0 / math.sqrt(conditions * height * wavenumbers)
    return (
        filtered.reshape(local_shape),
        totals[0] * normalizer,
        totals[1] * normalizer,
        totals[2] * normalizer,
        totals[3] * normalizer,
    )


def solution(mesh):
    placed = (P(None, "lat", "lon", None), P(None, None, "lon", "lat", None), P(), P(), P(), P())
    return jax.shard_map(
        per_device,
        mesh=mesh,
        in_specs=placed,
        out_specs=(P(None, None, "lon", "lat", None), P(), P(), P(), P()),
        check_vma=False,
    )
```

profile of v0, /device:TPU:0, one launch (start us, length us, event | category | flops | bytes accessed | tf_op | source)
XLA Modules:
  0.0 218.2 jit_solution(6437234970947821318)
XLA Ops:
  7.2 2.2 copy.51
  9.3 1.6 reshape.124
  10.9 10.5 %all_to_all.45 = bf16[4,2,12288]{2,1,0:T(2,128)(2,1)S(1)} all-to-all(bf16[4,2,12288]{2,1,0:T(2,128)(2,1)S(1)} %reshape.124), channel_id=1, replica_groups=mesh['lat'=4,'lon'=8] {'lat'}, dimensions={0} | all-to-all | bytes 393216 | tf_op jit(solution)/shard_map/all_to_all | solution.py:118
  21.4 1.2 reshape.125
  22.6 1.0 copy.52
  23.9 0.4 convolution_negate_fusion
  24.5 0.5 convolution_bitcast_fusion
  25.5 1.6 copy.55
  27.1 5.0 %all-to-all-start.1 = ((f32[2,1,64,8,192]{4,3,1,0,2:T(8,128)}), f32[2,1,64,8,192]{4,3,1,0,2:T(8,128)S(1)}, u32[]{:S(2)}, u32[]{:S(2)}) async-start(f32[2,1,64,8,192]{4,3,1,0,2:T(8,128)} %copy.55), calls=%async_computation.1 | async-start | bytes 2097152 | tf_op jit(solution)/shard_map/all_to_all | solution.py:126
  32.4 26.3 %all-to-all-done.1 = f32[2,1,64,8,192]{4,3,1,0,2:T(8,128)S(1)} async-done(((f32[2,1,64,8,192]{4,3,1,0,2:T(8,128)}), f32[2,1,64,8,192]{4,3,1,0,2:T(8,128)S(1)}, u32[]{:S(2)}, u32[]{:S(2)}) %all-to-all-start.1) | async-done | bytes 786464 | tf_op jit(solution)/shard_map/all_to_all | solution.py:126
  58.8 0.5 fusion.23
  59.2 0.5 fusion.22
  59.7 0.5 fusion.20
  60.2 0.5 fusion.21
  60.7 0.9 copy.57
  61.6 3.4 %all-to-all-start.2 = ((bf16[2,1,8,32,192]{4,2,1,0,3:T(8,128)(2,1)}), bf16[2,1,8,32,192]{4,2,1,0,3:T(8,128)(2,1)S(1)}, u32[]{:S(2)}, u32[]{:S(2)}) async-start(bf16[2,1,8,32,192]{4,2,1,0,3:T(8,128)(2,1)} %copy.57), calls=%async_computation.2 | async-start | bytes 524288 | tf_op jit(solution)/shard_map/all_to_all | solution.py:134
  65.2 5.2 %all-to-all-done.2 = bf16[2,1,8,32,192]{4,2,1,0,3:T(8,128)(2,1)S(1)} async-done(((bf16[2,1,8,32,192]{4,2,1,0,3:T(8,128)(2,1)}), bf16[2,1,8,32,192]{4,2,1,0,3:T(8,128)(2,1)S(1)}, u32[]{:S(2)}, u32[]{:S(2)}) %all-to-all-start.2) | async-done | bytes 196640 | tf_op jit(solution)/shard_map/all_to_all | solution.py:134
  76.1 0.9 pad_maximum_fusion.1
  77.0 0.9 pad_maximum_fusion.2
  78.6 37.5 %all-reduce = (f32[2,8,96]{2,1,0:T(8,128)S(1)}, f32[2,8,96]{2,1,0:T(8,128)S(1)}) all-reduce(f32[2,8,96]{2,1,0:T(8,128)S(1)} %pad_maximum_fusion.5, f32[2,8,96]{2,1,0:T(8,128)S(1)} %pad_maximum_fusion.6), channel_id=1, replica_groups=mesh['lat'=4,'lon'=8] {'lat','lon'}, use_global_device_ids=true, to_apply=%region_3.4 | all-reduce | flops 3072 | bytes 24576 | tf_op jit(solution)/shard_map/psum | solution.py:143
  116.1 0.8 pad_maximum_fusion.3
  116.9 0.6 broadcast_multiply_fusion.2
  117.5 91.3 %all-reduce.4.cloned.1.call-done = (f32[2,8,96,96]{3,2,1,0:T(8,128)}, f32[2,8,96,96]{3,2,1,0:T(8,128)}) async-done(((f32[2,8,96,96]{3,2,1,0:T(8,128)}, f32[2,8,96,96]{3,2,1,0:T(8,128)}), (f32[2,8,96,96]{3,2,1,0:T(8,128)}, f32[2,8,96,96]{3,2,1,0:T(8,128)})) %all-reduce.4.cloned.1.call-update) | async-done | bytes 1179664 | tf_op jit(solution)/shard_map/psum | solution.py:143
  208.7 2.7 %broadcast_multiply_fusion = (f32[2,8,96,96]{3,2,1,0:T(8,128)}, f32[2,8,96,96]{3,2,1,0:T(8,128)}) fusion(f32[2,8,96,96]{3,2,1,0:T(8,128)} %get-tuple-element.8, f32[2,8,96,96]{3,2,1,0:T(8,128)} %get-tuple-element.7), kind=kLoop, calls=%fused_computation.45 | loop fusion | flops 294912 | bytes 2359296 | tf_op jit(solution)/shard_map/mul | solution.py:149
  (54 shorter events, 7.7 us)
Async XLA Ops:
  27.0 5.0 %copy-start.2 = (bf16[2,1,8,8,768]{4,3,2,1,0:T(8,128)(2,1)S(1)}, bf16[2,1,8,8,768]{4,3,2,1,0:T(8,128)(2,1)}, u32[]{:S(2)}) copy-start(bf16[2,1,8,8,768]{4,3,2,1,0:T(8,128)(2,1)} %param.7) | copy-start | bytes 589828
  27.1 5.3 %copy-start.3 = (f32[2,8,96]{2,1,0:T(8,128)S(1)}, f32[2,8,96]{2,1,0:T(8,128)}, u32[]{:S(2)}) copy-start(f32[2,8,96]{2,1,0:T(8,128)} %param.9) | copy-start | bytes 18436
  27.1 31.6 %all-to-all-start.1 = ((f32[2,1,64,8,192]{4,3,1,0,2:T(8,128)}), f32[2,1,64,8,192]{4,3,1,0,2:T(8,128)S(1)}, u32[]{:S(2)}, u32[]{:S(2)}) async-start(f32[2,1,64,8,192]{4,3,1,0,2:T(8,128)} %copy.55), calls=%async_computation.1 | async-start | bytes 2097152 | tf_op jit(solution)/shard_map/all_to_all | solution.py:126
  59.7 5.5 %copy-start.4 = (f32[2,8,96]{2,1,0:T(8,128)S(1)}, f32[2,8,96]{2,1,0:T(8,128)}, u32[]{:S(2)}) copy-start(f32[2,8,96]{2,1,0:T(8,128)} %param.11) | copy-start | bytes 18436
  60.6 10.4 %copy-start.1 = (bf16[2,8,96,96]{3,2,1,0:T(8,128)(2,1)S(1)}, bf16[2,8,96,96]{3,2,1,0:T(8,128)(2,1)}, u32[]{:S(2)}) copy-start(bf16[2,8,96,96]{3,2,1,0:T(8,128)(2,1)} %param.8) | copy-start | bytes 884740
  61.6 8.8 %all-to-all-start.2 = ((bf16[2,1,8,32,192]{4,2,1,0,3:T(8,128)(2,1)}), bf16[2,1,8,32,192]{4,2,1,0,3:T(8,128)(2,1)S(1)}, u32[]{:S(2)}, u32[]{:S(2)}) async-start(bf16[2,1,8,32,192]{4,2,1,0,3:T(8,128)(2,1)} %copy.57), calls=%async_computation.2 | async-start | bytes 524288 | tf_op jit(solution)/shard_map/all_to_all | solution.py:134
  65.0 143.8 %all-reduce.4.cloned.1.call-start = ((), (), s32[]{:S(2)}) async-start(), calls=%async_computation.3 | async-start | bytes 3145728 | tf_op jit(solution)/shard_map/psum | solution.py:143
  70.6 1.1 copy-start
Sparse Core Ops, SparseCore 0:
  78.1 130.5 all-reduce.3
where the time goes:
time: 219 us; the launch traced here: 218 us
  waiting for transfers between devices  123 us (56%)
  blocking collectives  48 us (22%)
  between operations  14.4 us (7%)
  local copies, waits for them, and re-layouts  10.7 us (5%)
  starting transfers between devices  8.63 us (4%)
  matrix products  7.71 us (4%)
  other arithmetic  6.09 us (3%)
    psum x1, waiting for transfers between devices, per_device(): lax.psum((gradients[0], gradients[1], gradients[2], gradients[3]), ('lat'...  91.3 us
    psum x1, blocking collectives, per_device(): lax.psum((gradients[0], gradients[1], gradients[2], gradients[3]), ('lat'...  37.5 us
    all_to_all x1, waiting for transfers between devices, per_device(): lax.all_to_all(spec_rows, 'lon', split_axis=2, concat_axis=3, tiled=True)  26.3 us
    all_to_all x1, blocking collectives, per_device(): lax.all_to_all(fields, 'lat', split_axis=3, concat_axis=1, tiled=True)  10.5 us
    all_to_all x1, waiting for transfers between devices, per_device(): lax.all_to_all(spec_half, 'lat', split_axis=3, concat_axis=4, tiled=True)  5.17 us
    all_to_all x1, starting transfers between devices, per_device(): lax.all_to_all(spec_rows, 'lon', split_axis=2, concat_axis=3, tiled=True)  5 us
    unnamed x13, local copies, waits for them, and re-layouts  4.92 us
  transfers between devices with their start and end apart: 3, of which 3 were waited for; matrix products, arithmetic and copies ran while one was open for 1% of the time, Pallas kernels for 0%

commit v1 on v0

--- a/solution.py
+++ b/solution.py
@@ -140,7 +140,9 @@
     filtered, gradients = block_filter(
         flat_spec, flat_cot, inner_kernel, inner_offset, outer_kernel, outer_offset
     )
-    totals = lax.psum((gradients[0], gradients[1], gradients[2], gradients[3]), ("lat", "lon"))
+    totals = (gradients[0], gradients[1], gradients[2], gradients[3])
+    for mesh_axis in ("lon", "lat"):
+        totals = lax.psum(totals, mesh_axis)
     normalizer = 1.0 / math.sqrt(conditions * height * wavenumbers)
     return (
         filtered.reshape(local_shape),

time: 219 us -> 212 us (0.968)
  waiting for transfers between devices: 123 us -> 111 us
  blocking collectives: 48 us -> 52.5 us
    psum x1 -> x2, waiting for transfers between devices: 91.3 us -> 79.3 us  [per_device(): totals = lax.psum(totals, mesh_axis)]
    psum x1 -> x2, blocking collectives: 37.5 us -> 42 us  [per_device(): totals = lax.psum(totals, mesh_axis)]
    mul x0 -> x2, other arithmetic: none -> 2.76 us  [the longest x1 2.16 us: per_device(): totals[0] * normalizer]
    unnamed x13 -> x15, local copies, waits for them, and re-layouts: 4.92 us -> 4.93 us
  transfers between devices with their start and end apart: 3 -> 4, of which waited for: 3 -> 4; matrix products, arithmetic and copies ran while one was open for 1% -> 1% of each run, Pallas kernels for 0% -> 0%
where the time goes in v1:
time: 212 us; the launch traced here: 211 us
  waiting for transfers between devices  111 us (52%)
  blocking collectives  52.5 us (25%)
  between operations  14.4 us (7%)
  local copies, waits for them, and re-layouts  10.7 us (5%)
  starting transfers between devices  8.67 us (4%)
  matrix products  7.72 us (4%)
  other arithmetic  6.54 us (3%)
    psum x2, waiting for transfers between devices, per_device(): totals = lax.psum(totals, mesh_axis)  79.3 us
    psum x2, blocking collectives, per_device(): totals = lax.psum(totals, mesh_axis)  42 us
    all_to_all x1, waiting for transfers between devices, per_device(): lax.all_to_all(spec_rows, 'lon', split_axis=2, concat_axis=3, tiled=True)  26.3 us
    all_to_all x1, blocking collectives, per_device(): lax.all_to_all(fields, 'lat', split_axis=3, concat_axis=1, tiled=True)  10.5 us
    all_to_all x1, waiting for transfers between devices, per_device(): lax.all_to_all(spec_half, 'lat', split_axis=3, concat_axis=4, tiled=True)  5.15 us
    all_to_all x1, starting transfers between devices, per_device(): lax.all_to_all(spec_rows, 'lon', split_axis=2, concat_axis=3, tiled=True)  5 us
    unnamed x15, local copies, waits for them, and re-layouts  4.93 us
  transfers between devices with their start and end apart: 4, of which 4 were waited for; matrix products, arithmetic and copies ran while one was open for 1% of the time, Pallas kernels for 0%

profile of v1, /device:TPU:0, one launch (start us, length us, event | category | flops | bytes accessed | tf_op | source)
XLA Modules:
  0.0 211.3 jit_solution(12195307395256194388)
XLA Ops:
  7.2 2.2 %copy.51 = bf16[1,16,8,768]{1,2,0,3:T(8,128)(2,1)S(1)} copy(bf16[1,16,8,768]{3,2,1,0:T(8,128)(2,1)} %param.6) | data formatting | bytes 393216 | tf_op args[0]
  9.3 1.6 reshape.124
  10.9 10.5 %all_to_all.45 = bf16[4,2,12288]{2,1,0:T(2,128)(2,1)S(1)} all-to-all(bf16[4,2,12288]{2,1,0:T(2,128)(2,1)S(1)} %reshape.124), channel_id=1, replica_groups=mesh['lat'=4,'lon'=8] {'lat'}, dimensions={0} | all-to-all | bytes 393216 | tf_op jit(solution)/shard_map/all_to_all | solution.py:118
  21.4 1.2 reshape.125
  22.6 1.0 copy.52
  24.5 0.5 convolution_bitcast_fusion
  25.5 1.6 copy.55
  27.1 5.0 %all-to-all-start.1 = ((f32[2,1,64,8,192]{4,3,1,0,2:T(8,128)}), f32[2,1,64,8,192]{4,3,1,0,2:T(8,128)S(1)}, u32[]{:S(2)}, u32[]{:S(2)}) async-start(f32[2,1,64,8,192]{4,3,1,0,2:T(8,128)} %copy.55), calls=%async_computation.1 | async-start | bytes 2097152 | tf_op jit(solution)/shard_map/all_to_all | solution.py:126
  32.4 26.3 %all-to-all-done.1 = f32[2,1,64,8,192]{4,3,1,0,2:T(8,128)S(1)} async-done(((f32[2,1,64,8,192]{4,3,1,0,2:T(8,128)}), f32[2,1,64,8,192]{4,3,1,0,2:T(8,128)S(1)}, u32[]{:S(2)}, u32[]{:S(2)}) %all-to-all-start.1) | async-done | bytes 786464 | tf_op jit(solution)/shard_map/all_to_all | solution.py:126
  59.7 0.5 fusion.20
  60.2 0.5 fusion.21
  60.7 0.9 copy.57
  61.6 3.4 %all-to-all-start.2 = ((bf16[2,1,8,32,192]{4,2,1,0,3:T(8,128)(2,1)}), bf16[2,1,8,32,192]{4,2,1,0,3:T(8,128)(2,1)S(1)}, u32[]{:S(2)}, u32[]{:S(2)}) async-start(bf16[2,1,8,32,192]{4,2,1,0,3:T(8,128)(2,1)} %copy.57), calls=%async_computation.2 | async-start | bytes 524288 | tf_op jit(solution)/shard_map/all_to_all | solution.py:134
  65.3 5.1 %all-to-all-done.2 = bf16[2,1,8,32,192]{4,2,1,0,3:T(8,128)(2,1)S(1)} async-done(((bf16[2,1,8,32,192]{4,2,1,0,3:T(8,128)(2,1)}), bf16[2,1,8,32,192]{4,2,1,0,3:T(8,128)(2,1)S(1)}, u32[]{:S(2)}, u32[]{:S(2)}) %all-to-all-start.2) | async-done | bytes 196640 | tf_op jit(solution)/shard_map/all_to_all | solution.py:134
  76.1 1.3 pad_maximum_fusion.1
  77.4 60.2 %all-reduce.7.cloned.1.call-done = (f32[2,8,96,96]{3,2,1,0:T(8,128)}, f32[2,8,96,96]{3,2,1,0:T(8,128)}) async-done(((f32[2,8,96,96]{3,2,1,0:T(8,128)}, f32[2,8,96,96]{3,2,1,0:T(8,128)}), (f32[2,8,96,96]{3,2,1,0:T(8,128)}, f32[2,8,96,96]{3,2,1,0:T(8,128)})) %all-reduce.7.cloned.1.call-update) | async-done | bytes 1179664 | tf_op jit(solution)/shard_map/psum | solution.py:145
  138.3 25.9 %all-reduce = (f32[2,8,96]{2,1,0:T(8,128)S(1)}, f32[2,8,96]{2,1,0:T(8,128)S(1)}) all-reduce(f32[2,8,96]{2,1,0:T(8,128)S(1)} %get-tuple-element.37, f32[2,8,96]{2,1,0:T(8,128)S(1)} %get-tuple-element.38), channel_id=1, replica_groups=mesh['lat'=4,'lon'=8] {'lon'}, use_global_device_ids=true, to_apply=%region_4.5 | all-reduce | flops 3072 | bytes 24576 | tf_op jit(solution)/shard_map/psum | solution.py:145
  164.2 16.1 %all-reduce.2 = (f32[2,8,96]{2,1,0:T(8,128)S(1)}, f32[2,8,96]{2,1,0:T(8,128)S(1)}) all-reduce(f32[2,8,96]{2,1,0:T(8,128)S(1)} %get-tuple-element.5, f32[2,8,96]{2,1,0:T(8,128)S(1)} %get-tuple-element.6), channel_id=1, replica_groups=mesh['lat'=4,'lon'=8] {'lat'}, use_global_device_ids=true, to_apply=%region_5.6 | all-reduce | flops 3072 | bytes 24576 | tf_op jit(solution)/shard_map/psum | solution.py:145
  180.3 0.8 pad_maximum_fusion.3
  181.1 0.6 broadcast_multiply_fusion.3
  181.7 0.6 broadcast_multiply_fusion.2
  182.3 19.1 %all-reduce.9.cloned.1.call-done = (f32[2,8,96,96]{3,2,1,0:T(8,128)}, f32[2,8,96,96]{3,2,1,0:T(8,128)}) async-done(((f32[2,8,96,96]{3,2,1,0:T(8,128)}, f32[2,8,96,96]{3,2,1,0:T(8,128)}), (f32[2,8,96,96]{3,2,1,0:T(8,128)}, f32[2,8,96,96]{3,2,1,0:T(8,128)})) %all-reduce.9.cloned.1.call-update) | async-done | bytes 1179664 | tf_op jit(solution)/shard_map/psum | solution.py:145
  201.4 2.2 %broadcast_multiply_fusion.1 = f32[2,8,96,96]{3,2,1,0:T(8,128)} fusion(f32[2,8,96,96]{3,2,1,0:T(8,128)} %get-tuple-element.11), kind=kLoop, calls=%fused_computation.46 | loop fusion | flops 147456 | bytes 1179648 | tf_op jit(solution)/shard_map/mul | solution.py:149
  203.5 1.0 broadcast_multiply_fusion
  (60 shorter events, 9.1 us)
Async XLA Ops:
  27.1 5.0 %copy-start.3 = (bf16[2,1,8,8,768]{4,3,2,1,0:T(8,128)(2,1)S(1)}, bf16[2,1,8,8,768]{4,3,2,1,0:T(8,128)(2,1)}, u32[]{:S(2)}) copy-start(bf16[2,1,8,8,768]{4,3,2,1,0:T(8,128)(2,1)} %param.7) | copy-start | bytes 589828
  27.1 5.3 %copy-start.4 = (f32[2,8,96]{2,1,0:T(8,128)S(1)}, f32[2,8,96]{2,1,0:T(8,128)}, u32[]{:S(2)}) copy-start(f32[2,8,96]{2,1,0:T(8,128)} %param.9) | copy-start | bytes 18436
  27.1 31.6 %all-to-all-start.1 = ((f32[2,1,64,8,192]{4,3,1,0,2:T(8,128)}), f32[2,1,64,8,192]{4,3,1,0,2:T(8,128)S(1)}, u32[]{:S(2)}, u32[]{:S(2)}) async-start(f32[2,1,64,8,192]{4,3,1,0,2:T(8,128)} %copy.55), calls=%async_computation.1 | async-start | bytes 2097152 | tf_op jit(solution)/shard_map/all_to_all | solution.py:126
  59.7 5.5 %copy-start.5 = (f32[2,8,96]{2,1,0:T(8,128)S(1)}, f32[2,8,96]{2,1,0:T(8,128)}, u32[]{:S(2)}) copy-start(f32[2,8,96]{2,1,0:T(8,128)} %param.11) | copy-start | bytes 18436
  60.7 10.4 %copy-start.2 = (bf16[2,8,96,96]{3,2,1,0:T(8,128)(2,1)S(1)}, bf16[2,8,96,96]{3,2,1,0:T(8,128)(2,1)}, u32[]{:S(2)}) copy-start(bf16[2,8,96,96]{3,2,1,0:T(8,128)(2,1)} %param.8) | copy-start | bytes 884740
  61.6 8.8 %all-to-all-start.2 = ((bf16[2,1,8,32,192]{4,2,1,0,3:T(8,128)(2,1)}), bf16[2,1,8,32,192]{4,2,1,0,3:T(8,128)(2,1)S(1)}, u32[]{:S(2)}, u32[]{:S(2)}) async-start(bf16[2,1,8,32,192]{4,2,1,0,3:T(8,128)(2,1)} %copy.57), calls=%async_computation.2 | async-start | bytes 524288 | tf_op jit(solution)/shard_map/all_to_all | solution.py:134
  65.0 72.6 %all-reduce.7.cloned.1.call-start = ((), (), s32[]{:S(2)}) async-start(), calls=%async_computation.3 | async-start | bytes 3145728 | tf_op jit(solution)/shard_map/psum | solution.py:145
  70.6 1.1 copy-start
  77.4 124.0 %all-reduce.9.cloned.1.call-start = ((), (), s32[]{:S(2)}) async-start(), calls=%async_computation.4 | async-start | bytes 3145728 | tf_op jit(solution)/shard_map/psum | solution.py:145
  201.4 2.2 %copy-start.1 = (f32[2,8,96,96]{3,2,1,0:T(8,128)S(1)}, f32[2,8,96,96]{3,2,1,0:T(8,128)}, u32[]{:S(2)}) copy-start(f32[2,8,96,96]{3,2,1,0:T(8,128)} %get-tuple-element.12) | copy-start | bytes 1769476
Sparse Core Ops, SparseCore 0:
  77.5 60.0 all-reduce.6
  140.7 60.5 all-reduce.8
